TPU v7x, 32 devices: a whole 2x2x4 slice. The times are simulated.
32 devices in a mesh: row: 4 (over z), col: 8 (over y, x, core).
Axes of the slice: x: 2, y: 2, z: 4, core: 2. Of those that a mesh axis runs over, the one named last changes fastest.
Arguments:
- positions: float32 [3, 65536], P(None, ('row', 'col')), may hold values from 0 to 1
- masses: float32 [1, 65536], P(None, ('row', 'col')), may hold values from 2e-09 to 2e-08
- counts: int32 [1, 512], P(None, ('row', 'col')), may hold values from 32 to 128
- sources: int32 [512, 8], P(('row', 'col')), may hold values from 0 to 47, as said below
Outputs:
- accel: float32 [3, 65536], P(None, ('row', 'col'))
Inputs may be any that keep to these rules, and one draw needn't show every extreme that they name: `sources`: each device's source ids name exactly 4 distinct leaves of the lower row neighbour and exactly 4 of the upper one.
All inputs are finite; a program needn't handle non-finite values.
Results may differ from a plain program's by a relative error of at most 0.00024.
Values sent between devices are 32-bit elements; how exact they have to be, the bound alone decides.
A program may use at most 64 MiB of HBM per device.

v0:
```python
import functools

import jax
import jax.numpy as jnp
from jax import lax
from jax.experimental import pallas as pl
from jax.experimental.pallas import tpu as pltpu
from jax.sharding import PartitionSpec as P

softening = 2.5e-07
COMPONENTS = 4
CHUNK = 32
GROUP = 16
MESH = pl.DeviceIdType.MESH


def vmem_limit(leaves, width):
    return 8 * 2**20 + 12 * leaves * width * width


def exchange_kernel(
    rows, cols, pos_hbm, mass_hbm, counts_hbm, table, spread_targets,
    pos, mass, counts, packed, in_sems, own_sem, send, recv, up_send, down_send, low_recv, high_recv,
):
    r, c = lax.axis_index("row"), lax.axis_index("col")
    up, down = lax.rem(r + 1, rows), lax.rem(r + rows - 1, rows)
    loads = [
        pltpu.make_async_copy(src, dst, in_sems.at[i])
        for i, (src, dst) in enumerate(((pos_hbm, pos), (mass_hbm, mass), (counts_hbm, counts)))
    ]
    for load in loads:
        load.start()

    barrier = pltpu.get_barrier_semaphore()
    pl.semaphore_signal(barrier, inc=1, device_id=(up, c), device_id_type=MESH)
    pl.semaphore_signal(barrier, inc=1, device_id=(down, c), device_id_type=MESH)

    def greet(o, carry):
        peer = lax.rem(c + o, cols)
        pl.semaphore_signal(barrier, inc=1, device_id=(r, peer), device_id_type=MESH)
        return carry

    lax.fori_loop(1, cols, greet, 0)
    for load in loads:
        load.wait()

    tile = packed.shape[1]
    blk = tile // COMPONENTS
    width = packed.shape[2]
    lane = lax.broadcasted_iota(jnp.int32, (1, width), 1)

    def pack(p, carry):
        for b in range(blk):
            leaf = p * blk + b
            here = pl.ds(pl.multiple_of(leaf * width, width), width)
            packed[p, COMPONENTS * b : COMPONENTS * b + 3, :] = pos[:, here]
            packed[p, COMPONENTS * b + 3 : COMPONENTS * b + 4, :] = jnp.where(
                lane < counts[0, leaf], mass[:, here], 0.0
            )
        return carry

    lax.fori_loop(0, cols, pack, 0, unroll=cols <= 8)
    pl.semaphore_wait(barrier, cols + 1)

    def across(o):
        peer = lax.rem(c + o, cols)
        return pltpu.make_async_remote_copy(
            src_ref=packed.at[peer], dst_ref=table.at[0, c],
            send_sem=send.at[peer], recv_sem=recv.at[c],
            device_id=(r, peer), device_id_type=MESH,
        )

    def along(src, p, to_up):
        return pltpu.make_async_remote_copy(
            src_ref=src, dst_ref=table.at[1 if to_up else 2, p],
            send_sem=(up_send if to_up else down_send).at[p],
            recv_sem=(low_recv if to_up else high_recv).at[p],
            device_id=(up if to_up else down, c), device_id_type=MESH,
        )

    def send_across(o, carry):
        across(o).start()
        return carry

    lax.fori_loop(1, cols, send_across, 0)
    along(packed.at[c], c, True).start()
    along(packed.at[c], c, False).start()
    own = pltpu.make_async_copy(packed.at[c], table.at[0, c], own_sem)
    own.start()

    def forward(o, carry):
        p = lax.bitwise_xor(c, o) if cols & (cols - 1) == 0 else lax.rem(c + o, cols)
        pltpu.make_async_remote_copy(
            src_ref=packed.at[p], dst_ref=table.at[0, p],
            send_sem=send.at[p], recv_sem=recv.at[p],
            device_id=(r, p), device_id_type=MESH,
        ).wait_recv()
        along(table.at[0, p], p, True).start()
        along(table.at[0, p], p, False).start()
        return carry

    lax.fori_loop(1, cols, forward, 0)
    own.wait()

    def spread(p, carry):
        columns = table[0, p].T
        for b in range(blk):
            for axis in range(3):
                at = COMPONENTS * b + axis
                spread_targets[p * blk + b, axis] = jnp.broadcast_to(
                    columns[:, at : at + 1], (width, width)
                )
        return carry

    lax.fori_loop(0, cols, spread, 0, unroll=2)

    def settle_sends(o, carry):
        across(o).wait_send()
        return carry

    lax.fori_loop(1, cols, settle_sends, 0)

    def settle(p, carry):
        for to_up in (True, False):
            copy = along(table.at[0, p], p, to_up)
            copy.wait_send()
            copy.wait_recv()
        return carry

    lax.fori_loop(0, cols, settle, 0)


def exchange(rows, cols, positions, masses, counts):
    leaves = counts.shape[1]
    width = positions.shape[1] // leaves
    tile = COMPONENTS * (leaves // cols)
    dma = pltpu.SemaphoreType.DMA
    return pl.pallas_call(
        functools.partial(exchange_kernel, rows, cols),
        out_shape=(
            jax.ShapeDtypeStruct((3, cols, tile, width), jnp.float32),
            jax.ShapeDtypeStruct((leaves, 3, width, width), jnp.float32),
        ),
        in_specs=[pl.BlockSpec(memory_space=pltpu.HBM)] * 3,
        out_specs=(pl.BlockSpec(memory_space=pltpu.VMEM),) * 2,
        scratch_shapes=[
            pltpu.VMEM(positions.shape, jnp.float32),
            pltpu.VMEM(masses.shape, jnp.float32),
            pltpu.SMEM(counts.shape, jnp.int32),
            pltpu.VMEM((cols, tile, width), jnp.float32),
            dma((3,)), dma(()), dma((cols,)), dma((cols,)),
            dma((cols,)), dma((cols,)), dma((cols,)), dma((cols,)),
        ],
        compiler_params=pltpu.CompilerParams(collective_id=0, has_side_effects=True, vmem_limit_bytes=vmem_limit(leaves, width)),
        name="exchange",
    )(positions, masses, counts)


def row_sums(parts, lane, sublane):
    shift = 8
    while len(parts) > 1:
        second = (lane & shift) != 0
        parts = [
            jnp.where(second, b, a) + pltpu.roll(jnp.where(second, a, b), shift, 1)
            for a, b in zip(parts[::2], parts[1::2])
        ]
        shift *= 2
    (total,) = parts
    width = total.shape[1]
    for shift in (1, 2, 4):
        second = (lane & shift) != 0
        total = total + jnp.where(
            second, pltpu.roll(total, shift, 1), pltpu.roll(total, width - shift, 1)
        )
    return jnp.sum(jnp.where((lane & 7) == sublane, total, 0.0), axis=0, keepdims=True)


def force_kernel(sources_hbm, table, spread_targets, out, sources, pulls, live, in_sem):
    width = table.shape[1]
    group = pulls.shape[0]
    per_list = sources.shape[0]
    lane = lax.broadcasted_iota(jnp.int32, (8, width), 1)
    sublane = lax.broadcasted_iota(jnp.int32, (8, width), 0)
    load = pltpu.make_async_copy(sources_hbm, sources, in_sem)
    load.start()

    def one_group(g, carry):
        def count(i, carry):
            alive = table[pl.ds((g * group + i) * COMPONENTS + 3, 1), :] > 0.0
            live[i] = jnp.sum(alive.astype(jnp.int32))
            return carry

        lax.fori_loop(0, group, count, 0, unroll=True)

        @pl.when(g == 0)
        def _():
            load.wait()

        def one_target(i, carry):
            ids = [sources[k, g * group + i] * COMPONENTS for k in range(per_list)]

            def one_chunk(n, carry):
                here = pl.ds(pl.multiple_of(n * CHUNK, CHUNK), CHUNK)
                tx, ty, tz = (spread_targets[g * group + i, axis, here, :] for axis in range(3))
                ax = ay = az = jnp.zeros((CHUNK, width), jnp.float32)
                for k in range(per_list):
                    dx = table[pl.ds(ids[k], 1), :] - tx
                    dy = table[pl.ds(ids[k] + 1, 1), :] - ty
                    dz = table[pl.ds(ids[k] + 2, 1), :] - tz
                    inverse = lax.rsqrt(softening + dx * dx + dy * dy + dz * dz)
                    weight = table[pl.ds(ids[k] + 3, 1), :] * inverse * (inverse * inverse)
                    ax, ay, az = ax + weight * dx, ay + weight * dy, az + weight * dz
                pulls[i, 0, here, :] = ax
                pulls[i, 1, here, :] = ay
                pulls[i, 2, here, :] = az
                return carry

            chunks = lax.div(live[i] + (CHUNK - 1), CHUNK)
            return lax.fori_loop(0, chunks, one_chunk, carry)

        lax.fori_loop(0, group, one_target, 0)

        def reduce(i, carry):
            t = g * group + i
            alive = table[pl.ds(t * COMPONENTS + 3, 1), :] > 0.0
            for axis in range(3):
                parts = [pulls[i, axis, 8 * n : 8 * n + 8, :] for n in range(width // 8)]
                out[axis : axis + 1, pl.ds(pl.multiple_of(t * width, width), width)] = jnp.where(
                    alive, row_sums(parts, lane, sublane), 0.0
                )
            return carry

        lax.fori_loop(0, group, reduce, 0, unroll=8)
        return carry

    lax.fori_loop(0, sources.shape[1] // group, one_group, 0)


def forces(table, spread_targets, sources):
    leaves, width = sources.shape[1], table.shape[1]
    group = GROUP if leaves % GROUP == 0 else leaves
    return pl.pallas_call(
        force_kernel,
        out_shape=jax.ShapeDtypeStruct((3, leaves * width), jnp.float32),
        in_specs=[pl.BlockSpec(memory_space=pltpu.HBM)] + [pl.BlockSpec(memory_space=pltpu.VMEM)] * 2,
        out_specs=pl.BlockSpec(memory_space=pltpu.VMEM),
        scratch_shapes=[
            pltpu.SMEM(sources.shape, jnp.int32),
            pltpu.VMEM((group, 3, width, width), jnp.float32),
            pltpu.SMEM((group,), jnp.int32),
            pltpu.SemaphoreType.DMA(()),
        ],
        compiler_params=pltpu.CompilerParams(vmem_limit_bytes=vmem_limit(leaves, width)),
        name="forces",
    )(sources, table, spread_targets)


def in_hbm(array):
    return pltpu.with_memory_space_constraint(array, pltpu.HBM)


def solution(mesh):
    rows, cols = mesh.shape["row"], mesh.shape["col"]

    def on_device(positions, masses, counts, sources):
        table, spread_targets = exchange(rows, cols, *(in_hbm(a) for a in (positions, masses, counts)))
        return forces(table.reshape(-1, table.shape[-1]), spread_targets, in_hbm(sources.T))

    return jax.shard_map(
        on_device,
        mesh=mesh,
        in_specs=(
            P(None, ("row", "col")),
            P(None, ("row", "col")),
            P(None, ("row", "col")),
            P(("row", "col"), None),
        ),
        out_specs=P(None, ("row", "col")),
        check_vma=False,
    )
```

profile of v0, /device:TPU:0, one launch (start us, length us, event | category | flops | bytes accessed | tf_op | source)
XLA Modules:
  0.0 21.2 jit_solution(9174138973536482988)
XLA Ops:
  0.0 12.2 %exchange.1 = (f32[3,8,8,128]{3,2,1,0:T(8,128)S(1)}, f32[16,3,128,128]{3,2,1,0:T(8,128)S(1)}) custom-call(f32[3,2048]{1,0:T(4,128)} %pos_hbm.1, f32[1,2048]{1,0:T(1,128)} %mass_hbm.1, s32[1,16]{1,0:T(1,128)} %counts_hbm.1), custom_call_target="tpu_custom_call" | custom-call | tf_op jit(solution)/shard_map/exchange/pallas_call | solution.py:138
  12.3 9.0 %forces.1 = f32[3,2048]{1,0:T(4,128)} custom-call(s32[8,16]{1,0:T(8,128)} %bitcast.3, f32[192,128]{1,0:T(8,128)S(1)} %bitcast.2, f32[16,3,128,128]{3,2,1,0:T(8,128)S(1)} %get-tuple-element.8.spread_targets), custom_call_target="tpu_custom_call" | custom-call | tf_op jit(solution)/shard_map/forces/pallas_call | solution.py:242
where the time goes:
time: 21.4 us; the launch traced here: 21.2 us
  Pallas kernels  21.2 us (99%)
    pallas_call x1, Pallas kernels, exchange(): pl.pallas_call(functools.partial(exchange_kernel, rows, cols), out_shape=...  12.2 us
    pallas_call x1, Pallas kernels, forces(): pl.pallas_call(force_kernel, out_shape=jax.ShapeDtypeStruct((3, leaves *...  8.98 us

commit v1 on v0

--- a/solution.py
+++ b/solution.py
@@ -156,14 +156,27 @@
     )(positions, masses, counts)
 
 
-def row_sums(parts, lane, sublane):
+def merge(parts, shift, lane):
+    second = (lane & shift) != 0
+    return [
+        jnp.where(second, b, a) + pltpu.roll(jnp.where(second, a, b), shift, 1)
+        for a, b in zip(parts[::2], parts[1::2])
+    ]
+
+
+def merge_chunk(pull, lane):
+    parts = [pull[8 * n : 8 * n + 8] for n in range(CHUNK // 8)]
     shift = 8
     while len(parts) > 1:
-        second = (lane & shift) != 0
-        parts = [
-            jnp.where(second, b, a) + pltpu.roll(jnp.where(second, a, b), shift, 1)
-            for a, b in zip(parts[::2], parts[1::2])
-        ]
+        parts = merge(parts, shift, lane)
+        shift *= 2
+    return parts[0]
+
+
+def row_sums(parts, lane, sublane):
+    shift = CHUNK
+    while len(parts) > 1:
+        parts = merge(parts, shift, lane)
         shift *= 2
     (total,) = parts
     width = total.shape[1]
@@ -175,9 +188,10 @@
     return jnp.sum(jnp.where((lane & 7) == sublane, total, 0.0), axis=0, keepdims=True)
 
 
-def force_kernel(sources_hbm, table, spread_targets, out, sources, pulls, live, in_sem):
+def force_kernel(sources_hbm, table, spread_targets, out, sources, pull, merged, live, in_sem):
     width = table.shape[1]
-    group = pulls.shape[0]
+    group = live.shape[0]
+    per_leaf = width // CHUNK
     per_list = sources.shape[0]
     lane = lax.broadcasted_iota(jnp.int32, (8, width), 1)
     sublane = lax.broadcasted_iota(jnp.int32, (8, width), 0)
@@ -199,7 +213,9 @@
         def one_target(i, carry):
             ids = [sources[k, g * group + i] * COMPONENTS for k in range(per_list)]
 
-            def one_chunk(n, carry):
+            def one_chunk(n, before):
+                for axis in range(3):
+                    merged[before, axis] = merge_chunk(pull[axis], lane)
                 here = pl.ds(pl.multiple_of(n * CHUNK, CHUNK), CHUNK)
                 tx, ty, tz = (spread_targets[g * group + i, axis, here, :] for axis in range(3))
                 ax = ay = az = jnp.zeros((CHUNK, width), jnp.float32)
@@ -210,21 +226,21 @@
                     inverse = lax.rsqrt(softening + dx * dx + dy * dy + dz * dz)
                     weight = table[pl.ds(ids[k] + 3, 1), :] * inverse * (inverse * inverse)
                     ax, ay, az = ax + weight * dx, ay + weight * dy, az + weight * dz
-                pulls[i, 0, here, :] = ax
-                pulls[i, 1, here, :] = ay
-                pulls[i, 2, here, :] = az
-                return carry
+                pull[0], pull[1], pull[2] = ax, ay, az
+                return i * per_leaf + n
 
             chunks = lax.div(live[i] + (CHUNK - 1), CHUNK)
             return lax.fori_loop(0, chunks, one_chunk, carry)
 
-        lax.fori_loop(0, group, one_target, 0)
+        last = lax.fori_loop(0, group, one_target, group * per_leaf)
+        for axis in range(3):
+            merged[last, axis] = merge_chunk(pull[axis], lane)
 
         def reduce(i, carry):
             t = g * group + i
             alive = table[pl.ds(t * COMPONENTS + 3, 1), :] > 0.0
             for axis in range(3):
-                parts = [pulls[i, axis, 8 * n : 8 * n + 8, :] for n in range(width // 8)]
+                parts = [merged[i * per_leaf + n, axis] for n in range(per_leaf)]
                 out[axis : axis + 1, pl.ds(pl.multiple_of(t * width, width), width)] = jnp.where(
                     alive, row_sums(parts, lane, sublane), 0.0
                 )
@@ -246,7 +262,8 @@
         out_specs=pl.BlockSpec(memory_space=pltpu.VMEM),
         scratch_shapes=[
             pltpu.SMEM(sources.shape, jnp.int32),
-            pltpu.VMEM((group, 3, width, width), jnp.float32),
+            pltpu.VMEM((3, CHUNK, width), jnp.float32),
+            pltpu.VMEM((group * (width // CHUNK) + 1, 3, 8, width), jnp.float32),
             pltpu.SMEM((group,), jnp.int32),
             pltpu.SemaphoreType.DMA(()),
         ],

time: 21.4 us -> 22.1 us (1.033)
  Pallas kernels: 21.2 us -> 22 us
    pallas_call x1, Pallas kernels: 8.98 us -> 9.71 us  [forces(): pl.pallas_call(force_kernel, out_shape=jax.ShapeDtypeStruct((3, leaves *...]
where the time goes in v1:
time: 22.1 us; the launch traced here: 22 us
  Pallas kernels  22 us (100%)
    pallas_call x1, Pallas kernels, exchange(): pl.pallas_call(functools.partial(exchange_kernel, rows, cols), out_shape=...  12.2 us
    pallas_call x1, Pallas kernels, forces(): pl.pallas_call(force_kernel, out_shape=jax.ShapeDtypeStruct((3, leaves *...  9.71 us

profile of v1, /device:TPU:0, one launch (start us, length us, event | category | flops | bytes accessed | tf_op | source)
XLA Modules:
  0.0 22.0 jit_solution(2846180478405668067)
XLA Ops:
  0.0 12.2 %exchange.1 = (f32[3,8,8,128]{3,2,1,0:T(8,128)S(1)}, f32[16,3,128,128]{3,2,1,0:T(8,128)S(1)}) custom-call(f32[3,2048]{1,0:T(4,128)} %pos_hbm.1, f32[1,2048]{1,0:T(1,128)} %mass_hbm.1, s32[1,16]{1,0:T(1,128)} %counts_hbm.1), custom_call_target="tpu_custom_call" | custom-call | tf_op jit(solution)/shard_map/exchange/pallas_call | solution.py:138
  12.3 9.7 %forces.1 = f32[3,2048]{1,0:T(4,128)} custom-call(s32[8,16]{1,0:T(8,128)} %bitcast.3, f32[192,128]{1,0:T(8,128)S(1)} %bitcast.2, f32[16,3,128,128]{3,2,1,0:T(8,128)S(1)} %get-tuple-element.8.spread_targets), custom_call_target="tpu_custom_call" | custom-call | tf_op jit(solution)/shard_map/forces/pallas_call | solution.py:258
